TPU v7x, 1024 devices: a whole 4x8x16 slice. The times are simulated.
1024 devices in a mesh: grp: 8 (over z_lo), blk: 128 (over x, z_hi, y, core).
Axes of the slice: x: 4, y: 8, z: 16 (z_hi: 2, z_lo: 8; z = z_hi * 8 + z_lo), core: 2. Of those that a mesh axis runs over, the one named last changes fastest.
Arguments:
- velocity_coef: float32 [2, 2, 8, 512, 512], P(None, None, 'grp', 'blk'), may hold values from -24 to 24
- scalar_field: float32 [32, 2048, 2048], P('grp', 'blk'), may hold values from -3 to 8
- plane_offset: int32 [32], P('grp'), may hold values from 0 to 127, as said below
Outputs:
- velocity_next: float32 [2, 2, 8, 512, 512], P(None, None, 'grp', 'blk')
- scalar_next: float32 [32, 2048, 2048], P('grp', 'blk')
Inputs may be any that keep to these rules, and one draw needn't show every extreme that they name: Fine plane n lies at z = plane_offset[n] / 16 coarse plane spacings (periodic), with 4 n <= plane_offset[n] <= 4 n + 3.
All inputs are finite; a program needn't handle non-finite values.
Results may differ from a plain program's by a relative error of at most 0.0003.
Values sent between devices are 32-bit elements; how exact they have to be, the bound alone decides.
A program may use at most 64 MiB of HBM per device.

v0:
```python
import functools

import jax
import jax.numpy as jnp
import numpy as np
from jax import lax
from jax.experimental import pallas as pl
from jax.experimental.pallas import tpu as pltpu
from jax.sharding import PartitionSpec as P

TIME_STEP = 0.05
VISCOSITY = 0.5
STENCIL = (0.8, -0.2, 4.0 / 105.0, -1.0 / 280.0)
HIGHEST = lax.Precision.HIGHEST
MESH = pl.DeviceIdType.MESH
NV = 512
OUTER = 8
INNER = 16
BLOCKS = OUTER * INNER
F32 = jnp.float32


def tables():
    base = np.arange(128)
    angle = 2.0 * np.pi * ((base[:, None] * base[None, :]) % 128) / 128.0
    table = np.concatenate([np.cos(angle), np.sin(angle)], 1)
    wave = np.arange(NV)
    signed = np.where(2 * wave < NV, wave, wave - NV)
    wavenum = 2.0 * np.pi * signed / NV
    rows = np.arange(8) - 1
    ang_x = 2.0 * np.pi * ((rows[:, None] * wave[None, :]) % NV) / NV
    cos_x, sin_x = np.cos(ang_x) / NV, np.sin(ang_x) / NV
    send = np.stack([cos_x, sin_x, -wavenum * sin_x, wavenum * cos_x], 0)
    digit = np.arange(4)
    ang_d = 2.0 * np.pi * ((digit[:, None] * wave[None, :]) % NV) / NV
    turn = np.stack([np.cos(ang_d), np.sin(ang_d)], 0)
    lane_digit = (np.arange(128) // 16) % 4
    ky = 4 * base[:, None] + lane_digit[None, :]
    weight = wavenum[ky]
    as32 = lambda a: np.asarray(a, np.float32)
    return as32(table), as32(send), as32(turn), as32(weight)


def exchange(sent, passed, landed, sems, blk, grp):
    outer, inner = blk // INNER, blk % INNER

    own = pltpu.make_async_copy(sent.at[outer], passed.at[outer], sems.at[0])
    own.start()

    def first(k, carry):
        there = lax.rem(outer + k, OUTER)
        pltpu.make_async_remote_copy(
            sent.at[there], passed.at[outer], sems.at[1], sems.at[2],
            device_id=(grp, there * INNER + inner), device_id_type=MESH,
        ).start()
        return carry

    lax.fori_loop(1, OUTER, first, 0)

    def rest():
        some = pl.ds(0, OUTER - 1)
        every = pltpu.make_async_remote_copy(
            sent.at[some], passed.at[some], sems.at[1], sems.at[2],
            device_id=(grp, lax.rem(outer + 1, OUTER) * INNER + inner), device_id_type=MESH,
        )
        own.wait()
        every.wait_recv()
        mine = pltpu.make_async_copy(passed.at[:, inner], landed.at[:, inner], sems.at[3])
        mine.start()

        def second(k, carry):
            there = lax.rem(inner + k, INNER)
            pltpu.make_async_remote_copy(
                passed.at[:, there], landed.at[:, inner], sems.at[4], sems.at[5],
                device_id=(grp, outer * INNER + there), device_id_type=MESH,
            ).start()
            return carry

        lax.fori_loop(1, INNER, second, 0)
        every.wait_send()

        def finish():
            part = pl.ds(0, INNER - 1)
            whole = pltpu.make_async_remote_copy(
                passed.at[:, part], landed.at[:, part], sems.at[4], sems.at[5],
                device_id=(grp, outer * INNER + lax.rem(inner + 1, INNER)), device_id_type=MESH,
            )
            mine.wait()
            whole.wait_recv()
            whole.wait_send()

        return finish

    return rest


def spectral_kernel(
    coef, scalar, table, send, turn, weight,
    next_coef, velocity, above, low, high,
    pack, sent, passed, landed, pack2, sent2, passed2, landed2,
    sems, sems2, halo_sems, grp_sems,
):
    blk = lax.axis_index("blk")
    grp = lax.axis_index("grp")
    outer, inner = blk // INNER, blk % INNER
    behind, ahead = lax.rem(blk + BLOCKS - 1, BLOCKS), lax.rem(blk + 1, BLOCKS)
    groups = lax.axis_size("grp")
    below, upper = lax.rem(grp + groups - 1, groups), lax.rem(grp + 1, groups)

    barrier = pltpu.get_barrier_semaphore()

    def hello(device):
        pl.semaphore_signal(barrier, inc=1, device_id=device, device_id_type=MESH)

    def greet_outer(k, carry):
        hello((grp, lax.rem(outer + k, OUTER) * INNER + inner))
        return carry

    def greet_inner(k, carry):
        hello((grp, outer * INNER + lax.rem(inner + k, INNER)))
        return carry

    lax.fori_loop(1, OUTER, greet_outer, 0)
    lax.fori_loop(1, INNER, greet_inner, 0)
    hello((grp, behind))
    hello((grp, ahead))
    hello((upper, blk))

    real = jnp.concatenate([coef[0, 0, 0], coef[1, 0, 0]], 0)
    imag = jnp.concatenate([coef[0, 1, 0], coef[1, 1, 0]], 0)
    for row in range(8):
        for kind in range(2):
            re, im = 0.0, 0.0
            for digit in range(4):
                lanes = slice(128 * digit, 128 * digit + 128)
                tr = send[2 * kind, row : row + 1, lanes]
                ti = send[2 * kind + 1, row : row + 1, lanes]
                re = re + (tr * real[:, lanes] - ti * imag[:, lanes])
                im = im + (tr * imag[:, lanes] + ti * real[:, lanes])
            start = 128 * kind + row
            pack[0, pl.ds(start, 8, 16), :] = re
            pack[1, pl.ds(start, 8, 16), :] = -im
            pack[0, pl.ds(start + 8, 8, 16), :] = im
            pack[1, pl.ds(start + 8, 8, 16), :] = re
    along_x = lax.dot_general(
        table[...], jnp.concatenate([pack[0], pack[1]], 1), (((1,), (1,)), ((), ())), precision=HIGHEST,
        preferred_element_type=F32,
    )
    for part in range(OUTER):
        rows = slice(part * INNER, part * INNER + INNER)
        sent[part, :, 0, :] = along_x[rows, 0:128]
        sent[part, :, 1, :] = along_x[rows, 128:256]

    pl.semaphore_wait(barrier, OUTER - 1 + INNER - 1 + 3)

    step = exchange(sent, passed, landed, sems, blk, grp)
    halos = []
    for plane in range(4):
        halos.append(pltpu.make_async_remote_copy(
            scalar.at[plane, pl.ds(8, 8)], low.at[plane],
            halo_sems.at[0, plane], halo_sems.at[1, plane],
            device_id=(grp, ahead), device_id_type=MESH,
        ))
        halos.append(pltpu.make_async_remote_copy(
            scalar.at[plane, pl.ds(0, 8)], high.at[plane],
            halo_sems.at[2, plane], halo_sems.at[3, plane],
            device_id=(grp, behind), device_id_type=MESH,
        ))
    for copy in halos:
        copy.start()
    step()()

    vel_in = jnp.concatenate([landed[part, :, 0, :] for part in range(OUTER)], 0)
    der_in = jnp.concatenate([landed[part, :, 1, :] for part in range(OUTER)], 0)
    stacked = jnp.concatenate([vel_in.T, (vel_in * weight[...]).T, der_in.T], 0)
    along_y = jnp.dot(stacked, table[...], precision=HIGHEST, preferred_element_type=F32)

    def synthesize(kind, component):
        parts = [0.0] * 4
        for digit in range(4):
            start = 128 * kind + (component * 4 + digit) * 16
            cos_re = along_y[start : start + 8, 0:128]
            sin_re = along_y[start : start + 8, 128:256]
            cos_im = along_y[start + 8 : start + 16, 0:128]
            sin_im = along_y[start + 8 : start + 16, 128:256]
            if kind == 1:
                head_re, head_im = -cos_im - sin_re, cos_re - sin_im
            else:
                head_re, head_im = cos_re - sin_im, sin_re + cos_im
            for part in range(4):
                lanes = slice(128 * part, 128 * part + 128)
                tr = turn[0, digit : digit + 1, lanes]
                ti = turn[1, digit : digit + 1, lanes]
                parts[part] = parts[part] + (tr * head_re - ti * head_im)
        return parts

    vel = [synthesize(0, 0), synthesize(0, 1)]
    for component in range(2):
        for part in range(4):
            velocity[component, :, 128 * part : 128 * part + 128] = vel[component][part]
    lift = pltpu.make_async_remote_copy(
        velocity, above, grp_sems.at[0], grp_sems.at[1],
        device_id=(below, blk), device_id_type=MESH,
    )
    lift.start()

    for component in range(2):
        grad_y = synthesize(1, component)
        grad_x = synthesize(2, component)
        adv = [vel[0][a] * grad_x[a] + vel[1][a] * grad_y[a] for a in range(4)]
        even, odd = adv[0] + adv[2], adv[1] + adv[3]
        even_d, odd_d = adv[0] - adv[2], adv[1] - adv[3]
        heads = [(even + odd, None), (even_d, -odd_d), (even - odd, None), (even_d, odd_d)]
        for digit, (p, q) in enumerate(heads):
            tr = turn[0, digit : digit + 1, 0:128]
            ti = turn[1, digit : digit + 1, 0:128]
            if q is None:
                re, im = p * tr, -(p * ti)
            else:
                re, im = p * tr + q * ti, q * tr - p * ti
            start = component * 4 + digit
            pack2[0, pl.ds(start, 8, 16), :] = re
            pack2[1, pl.ds(start, 8, 16), :] = im
            pack2[0, pl.ds(start + 8, 8, 16), :] = im
            pack2[1, pl.ds(start + 8, 8, 16), :] = -re
    forward_y = lax.dot_general(
        table[...], jnp.concatenate([pack2[0], pack2[1]], 1), (((1,), (1,)), ((), ())), precision=HIGHEST,
        preferred_element_type=F32,
    )
    for part in range(OUTER):
        sent2[part, :, 0, :] = forward_y[part * INNER : part * INNER + INNER]
    exchange(sent2, passed2, landed2, sems2, blk, grp)()()

    back = jnp.concatenate([landed2[part, :, 0, :] for part in range(OUTER)], 0)
    along = jnp.dot(back.T, table[...], precision=HIGHEST, preferred_element_type=F32)
    heads = []
    for row in range(1, 5):
        start = row * 16
        cos_re = along[start : start + 8, 0:128]
        sin_re = along[start : start + 8, 128:256]
        cos_im = along[start + 8 : start + 16, 0:128]
        sin_im = along[start + 8 : start + 16, 128:256]
        heads.append((cos_re + sin_im, cos_im - sin_re))
    row_index = lax.broadcasted_iota(jnp.int32, (8, 128), 0) % 4 + blk * 4
    row_signed = jnp.where(2 * row_index < NV, row_index, row_index - NV)
    row_wave = row_signed.astype(F32) * (2.0 * np.pi / NV)
    lane = lax.broadcasted_iota(jnp.int32, (8, 128), 1)
    for part in range(4):
        lanes = slice(128 * part, 128 * part + 128)
        re, im = 0.0, 0.0
        for digit, (head_re, head_im) in enumerate(heads):
            tr = turn[0, digit : digit + 1, lanes]
            ti = turn[1, digit : digit + 1, lanes]
            re = re + (tr * head_re + ti * head_im)
            im = im + (tr * head_im - ti * head_re)
        column = lane + 128 * part
        column_signed = column if part < 2 else column - NV
        column_wave = column_signed.astype(F32) * (2.0 * np.pi / NV)
        keep = (3 * jnp.abs(row_signed) < NV) & (3 * jnp.abs(column_signed) < NV)
        gain = jnp.where(keep, TIME_STEP / NV, 0.0)
        damping = jnp.exp(-VISCOSITY * TIME_STEP * (row_wave * row_wave + column_wave * column_wave))
        new_re = damping * (real[:, lanes] - gain * re)
        new_im = damping * (imag[:, lanes] - gain * im)
        for component in range(2):
            rows = slice(4 * component, 4 * component + 4)
            next_coef[component, 0, 0, :, lanes] = new_re[rows]
            next_coef[component, 1, 0, :, lanes] = new_im[rows]

    lift.wait()
    for copy in halos:
        copy.wait()


PAD = 128
NF = 2048
SPAN = 512


def transport_kernel(offset, scalar, low, high, velocity, above, spread, out, field, first, fine_y, flow):
    def place(buffer, rows, plane, value):
        buffer[plane, rows, PAD : PAD + NF] = value
        buffer[plane, rows, 0:PAD] = value[:, NF - PAD :]
        buffer[plane, rows, PAD + NF :] = value[:, :PAD]

    for plane in range(4):
        fraction = (offset[plane] % 16).astype(F32) * 0.0625
        for component in range(2):
            mixed = (1.0 - fraction) * velocity[component] + fraction * above[component]
            wide = jnp.concatenate([mixed, mixed[:, :128]], 1)
            rows = jnp.concatenate([wide[:, 128 * m : 128 * m + 256] for m in range(4)], 0)
            top = rows.astype(jnp.bfloat16)
            rest = (rows - top.astype(F32)).astype(jnp.bfloat16)
            fine_y[plane, component] = jnp.dot(
                top, spread[...], preferred_element_type=F32
            ) + jnp.dot(rest, spread[...], preferred_element_type=F32)

    index = lax.broadcasted_iota(jnp.int32, (8, 128), 0)
    share = (index % 4).astype(F32) * 0.25
    half = index < 4
    share_a = jnp.where(half, 1.0 - share, 0.0)
    share_b = jnp.where(half, share, 1.0 - share)
    share_c = jnp.where(half, 0.0, share)

    def wide_weights(value):
        return jnp.concatenate([value] * (SPAN // 128), 1)

    share_a, share_b, share_c = wide_weights(share_a), wide_weights(share_b), wide_weights(share_c)

    def along(values, axis):
        size = values.shape[axis]
        total = 0.0
        for offset_m, weight in zip((1, 2, 3, 4), STENCIL):
            total = total + (TIME_STEP * 4.0 * weight) * (
                pltpu.roll(values, size - offset_m, axis) - pltpu.roll(values, offset_m, axis)
            )
        return total

    def plane_step(plane, carry):
        place(field, slice(0, 8), plane, low[plane])
        place(field, slice(8, 24), plane, scalar[plane])
        place(field, slice(24, 32), plane, high[plane])
        for m in range(4):
            lanes = slice(SPAN * m, SPAN * m + SPAN)
            window = field[plane, :, SPAN * m : SPAN * m + SPAN + 2 * PAD]
            center = window[:, PAD : PAD + SPAN]
            dx = along(center, 0)
            dy = along(window, 1)[:, PAD : PAD + SPAN]
            speeds = []
            for component in range(2):
                tiles = []
                for tile in range(4):
                    bc = lambda j: jnp.broadcast_to(
                        fine_y[plane, component, 8 * m + j : 8 * m + j + 1, :], (8, SPAN)
                    )
                    tiles.append(
                        share_a * bc(max(2 * tile - 1, 0))
                        + share_b * bc(2 * tile)
                        + share_c * bc(2 * tile + 1)
                    )
                flow[component, :, lanes] = jnp.concatenate(tiles[1:3], 0)
                speeds.append(jnp.concatenate(tiles, 0))
            value = center - (speeds[0] * dx + speeds[1] * dy)
            first[:, PAD + SPAN * m : PAD + SPAN * m + SPAN] = value
            if m == 0:
                first[:, PAD + NF :] = value[:, :PAD]
            if m == 3:
                first[:, 0:PAD] = value[:, SPAN - PAD :]
        for m in range(4):
            lanes = slice(SPAN * m, SPAN * m + SPAN)
            window = first[:, SPAN * m : SPAN * m + SPAN + 2 * PAD]
            center = window[:, PAD : PAD + SPAN]
            dx = along(center, 0)[8:24]
            dy = along(window[8:24], 1)[:, PAD : PAD + SPAN]
            out[plane, :, lanes] = 0.5 * (
                (scalar[plane, :, lanes] + center[8:24])
                - (flow[0, :, lanes] * dx + flow[1, :, lanes] * dy)
            )
        return carry

    lax.fori_loop(0, 4, plane_step, 0)


def spread_table():
    fine = np.arange(512)
    table = np.zeros((256, 512), np.float32)
    table[fine // 4, fine] += 1.0 - (fine % 4) / 4.0
    table[fine // 4 + 1, fine] += (fine % 4) / 4.0
    return table


def vmem():
    return pl.BlockSpec(memory_space=pltpu.VMEM)


def body(velocity_coef, scalar_field, plane_offset):
    table, send, turn, weight = tables()
    dma = pltpu.SemaphoreType.DMA
    blocks = (OUTER, INNER)
    next_coef, velocity, above, low, high = pl.pallas_call(
        spectral_kernel,
        out_shape=(
            jax.ShapeDtypeStruct(velocity_coef.shape, F32),
            jax.ShapeDtypeStruct((2, 8, NV), F32),
            jax.ShapeDtypeStruct((2, 8, NV), F32),
            jax.ShapeDtypeStruct((4, 8, NF), F32),
            jax.ShapeDtypeStruct((4, 8, NF), F32),
        ),
        in_specs=[vmem()] * 6,
        out_specs=tuple([vmem()] * 5),
        scratch_shapes=[
            pltpu.VMEM((2, 256, 128), F32),
            pltpu.VMEM(blocks + (2, 128), F32),
            pltpu.VMEM(blocks + (2, 128), F32),
            pltpu.VMEM(blocks + (2, 128), F32),
            pltpu.VMEM((2, 128, 128), F32),
            pltpu.VMEM(blocks + (1, 128), F32),
            pltpu.VMEM(blocks + (1, 128), F32),
            pltpu.VMEM(blocks + (1, 128), F32),
            dma((6,)),
            dma((6,)),
            dma((4, 4)),
            dma((2,)),
        ],
        compiler_params=pltpu.CompilerParams(collective_id=0, has_side_effects=True),
        name="spectral",
    )(velocity_coef, scalar_field, jnp.asarray(table), jnp.asarray(send), jnp.asarray(turn), jnp.asarray(weight))
    scalar_next = pl.pallas_call(
        transport_kernel,
        out_shape=jax.ShapeDtypeStruct(scalar_field.shape, F32),
        in_specs=[pl.BlockSpec(memory_space=pltpu.SMEM)] + [vmem()] * 6,
        out_specs=vmem(),
        scratch_shapes=[
            pltpu.VMEM((4, 32, NF + 2 * PAD), F32),
            pltpu.VMEM((32, NF + 2 * PAD), F32),
            pltpu.VMEM((4, 2, 32, 512), F32),
            pltpu.VMEM((2, 16, NF), F32),
        ],
        name="transport",
    )(plane_offset, scalar_field, low, high, velocity, above, jnp.asarray(spread_table(), jnp.bfloat16))
    return next_coef, scalar_next


def solution(mesh):
    in_specs = (P(None, None, "grp", "blk", None), P("grp", "blk", None), P("grp"))
    out_specs = (P(None, None, "grp", "blk", None), P("grp", "blk", None))
    return jax.shard_map(body, mesh=mesh, in_specs=in_specs, out_specs=out_specs, check_vma=False)
```

profile of v0, /device:TPU:65, one launch (start us, length us, event | category | flops | bytes accessed | tf_op | source)
XLA Modules:
  0.0 69.3 jit_solution(15620676746150588682)
XLA Ops:
  0.6 60.2 %spectral.1 = (f32[2,2,1,4,512]{4,3,2,1,0:T(4,128)}, f32[2,8,512]{2,1,0:T(8,128)}, f32[2,8,512]{2,1,0:T(8,128)}, f32[4,8,2048]{2,1,0:T(8,128)}, f32[4,8,2048]{2,1,0:T(8,128)}) custom-call(f32[2,2,1,4,512]{4,3,2,1,0:T(4,128)} %coef.1, f32[4,16,2048]{2,1,0:T(8,128)} %scalar.3, f32[128,256]{1,0:T(8,128)} %constant.10.clone.table, ...), custom_call_target="tpu_custom_call" | custom-call | tf_op jit(solution)/shard_map/spectral/pallas_call | solution.py:379
  60.8 0.0 copy-start
  60.8 7.9 %transport.1 = f32[4,16,2048]{2,1,0:T(8,128)} custom-call(s32[4]{0:T(128)} %offset.1, f32[4,16,2048]{2,1,0:T(8,128)} %scalar.3, f32[4,8,2048]{2,1,0:T(8,128)} %get-tuple-element.8.low, f32[4,8,2048]{2,1,0:T(8,128)} %get-tuple-element.9.high, f32[2,8,512]{2,1,0:T(8,128)} %get-tuple-element.10.velocity, f32[2,8,512]{2,1,0:T(8,128)} %get-tuple-element.11.above, ...), custom_call_target="tpu_custom_call" | custom-call | tf_op jit(solution)/shard_map/transport/pallas_call | solution.py:407
  68.7 0.0 copy-done
  68.7 0.6 copy.11
Async XLA Ops:
  60.8 7.9 %copy-start = (f32[2,2,1,4,512]{4,3,2,1,0:T(4,128)S(1)}, f32[2,2,1,4,512]{4,3,2,1,0:T(4,128)}, u32[]{:S(2)}) copy-start(f32[2,2,1,4,512]{4,3,2,1,0:T(4,128)} %get-tuple-element.14) | copy-start | bytes 98308
where the time goes:
time: 69.5 us; the launch traced here: 69.3 us
  Pallas kernels  68 us (98%)
    pallas_call x1, Pallas kernels, body(): pl.pallas_call(spectral_kernel, out_shape=(jax.ShapeDtypeStruct(velocity_...  60.2 us
    pallas_call x1, Pallas kernels, body(): pl.pallas_call(transport_kernel, out_shape=jax.ShapeDtypeStruct(scalar_fi...  7.85 us

commit v1 on v0

--- a/solution.py
+++ b/solution.py
@@ -18,6 +18,9 @@
 INNER = 16
 BLOCKS = OUTER * INNER
 F32 = jnp.float32
+PAD = 128
+NF = 2048
+SPAN = 512
 
 
 def tables():
@@ -94,11 +97,12 @@
     return rest
 
 
-def spectral_kernel(
-    coef, scalar, table, send, turn, weight,
-    next_coef, velocity, above, low, high,
+def step_kernel(
+    offset, coef, scalar, table, send, turn, weight, spread,
+    next_coef, out,
     pack, sent, passed, landed, pack2, sent2, passed2, landed2,
-    sems, sems2, halo_sems, grp_sems,
+    velocity, above, field, slope, first, fine_y, flow,
+    sems, sems2, halo_sems, grp_sems, own_sem,
 ):
     blk = lax.axis_index("blk")
     grp = lax.axis_index("grp")
@@ -120,11 +124,20 @@
         hello((grp, outer * INNER + lax.rem(inner + k, INNER)))
         return carry
 
-    lax.fori_loop(1, OUTER, greet_outer, 0)
-    lax.fori_loop(1, INNER, greet_inner, 0)
     hello((grp, behind))
     hello((grp, ahead))
     hello((upper, blk))
+    lax.fori_loop(1, OUTER, greet_outer, 0)
+    lax.fori_loop(1, INNER, greet_inner, 0)
+    whole = pl.ds(PAD, NF)
+    own = [
+        pltpu.make_async_copy(
+            scalar.at[plane], field.at[plane, pl.ds(8, 16), whole], own_sem.at[plane]
+        )
+        for plane in range(4)
+    ]
+    for copy in own:
+        copy.start()
 
     real = jnp.concatenate([coef[0, 0, 0], coef[1, 0, 0]], 0)
     imag = jnp.concatenate([coef[0, 1, 0], coef[1, 1, 0]], 0)
@@ -157,12 +170,12 @@
     halos = []
     for plane in range(4):
         halos.append(pltpu.make_async_remote_copy(
-            scalar.at[plane, pl.ds(8, 8)], low.at[plane],
+            scalar.at[plane, pl.ds(8, 8)], field.at[plane, pl.ds(0, 8), whole],
             halo_sems.at[0, plane], halo_sems.at[1, plane],
             device_id=(grp, ahead), device_id_type=MESH,
         ))
         halos.append(pltpu.make_async_remote_copy(
-            scalar.at[plane, pl.ds(0, 8)], high.at[plane],
+            scalar.at[plane, pl.ds(0, 8)], field.at[plane, pl.ds(24, 8), whole],
             halo_sems.at[2, plane], halo_sems.at[3, plane],
             device_id=(grp, behind), device_id_type=MESH,
         ))
@@ -229,7 +242,15 @@
     )
     for part in range(OUTER):
         sent2[part, :, 0, :] = forward_y[part * INNER : part * INNER + INNER]
-    exchange(sent2, passed2, landed2, sems2, blk, grp)()()
+    step = exchange(sent2, passed2, landed2, sems2, blk, grp)
+    for copy in own + halos:
+        copy.wait()
+    lax.fori_loop(0, 4, functools.partial(slopes, field, slope), 0)
+    finish = step()
+    lift.wait()
+    refine_along_y(offset, velocity, above, spread, fine_y)
+    lax.fori_loop(0, 4, functools.partial(sections, field, slope, first, fine_y, flow, out), 0)
+    finish()
 
     back = jnp.concatenate([landed2[part, :, 0, :] for part in range(OUTER)], 0)
     along = jnp.dot(back.T, table[...], precision=HIGHEST, preferred_element_type=F32)
@@ -266,22 +287,7 @@
             next_coef[component, 0, 0, :, lanes] = new_re[rows]
             next_coef[component, 1, 0, :, lanes] = new_im[rows]
 
-    lift.wait()
-    for copy in halos:
-        copy.wait()
-
-
-PAD = 128
-NF = 2048
-SPAN = 512
-
-
-def transport_kernel(offset, scalar, low, high, velocity, above, spread, out, field, first, fine_y, flow):
-    def place(buffer, rows, plane, value):
-        buffer[plane, rows, PAD : PAD + NF] = value
-        buffer[plane, rows, 0:PAD] = value[:, NF - PAD :]
-        buffer[plane, rows, PAD + NF :] = value[:, :PAD]
-
+def refine_along_y(offset, velocity, above, spread, fine_y):
     for plane in range(4):
         fraction = (offset[plane] % 16).astype(F32) * 0.0625
         for component in range(2):
@@ -294,70 +300,71 @@
                 top, spread[...], preferred_element_type=F32
             ) + jnp.dot(rest, spread[...], preferred_element_type=F32)
 
-    index = lax.broadcasted_iota(jnp.int32, (8, 128), 0)
+
+def along(values, axis):
+    size = values.shape[axis]
+    total = 0.0
+    for shift, weight in zip((1, 2, 3, 4), STENCIL):
+        total = total + (TIME_STEP * 4.0 * weight) * (
+            pltpu.roll(values, size - shift, axis) - pltpu.roll(values, shift, axis)
+        )
+    return total
+
+
+def slopes(field, slope, plane, carry):
+    field[plane, :, 0:PAD] = field[plane, :, NF : NF + PAD]
+    field[plane, :, PAD + NF : NF + 2 * PAD] = field[plane, :, PAD : 2 * PAD]
+    for m in range(4):
+        lanes = slice(SPAN * m, SPAN * m + SPAN)
+        window = field[plane, :, SPAN * m : SPAN * m + SPAN + 2 * PAD]
+        slope[plane, 0, :, lanes] = along(window[:, PAD : PAD + SPAN], 0)
+        slope[plane, 1, :, lanes] = along(window, 1)[:, PAD : PAD + SPAN]
+    return carry
+
+
+def sections(field, slope, first, fine_y, flow, out, plane, carry):
+    index = lax.broadcasted_iota(jnp.int32, (8, SPAN), 0)
     share = (index % 4).astype(F32) * 0.25
     half = index < 4
     share_a = jnp.where(half, 1.0 - share, 0.0)
     share_b = jnp.where(half, share, 1.0 - share)
     share_c = jnp.where(half, 0.0, share)
-
-    def wide_weights(value):
-        return jnp.concatenate([value] * (SPAN // 128), 1)
-
-    share_a, share_b, share_c = wide_weights(share_a), wide_weights(share_b), wide_weights(share_c)
-
-    def along(values, axis):
-        size = values.shape[axis]
-        total = 0.0
-        for offset_m, weight in zip((1, 2, 3, 4), STENCIL):
-            total = total + (TIME_STEP * 4.0 * weight) * (
-                pltpu.roll(values, size - offset_m, axis) - pltpu.roll(values, offset_m, axis)
-            )
-        return total
-
-    def plane_step(plane, carry):
-        place(field, slice(0, 8), plane, low[plane])
-        place(field, slice(8, 24), plane, scalar[plane])
-        place(field, slice(24, 32), plane, high[plane])
-        for m in range(4):
-            lanes = slice(SPAN * m, SPAN * m + SPAN)
-            window = field[plane, :, SPAN * m : SPAN * m + SPAN + 2 * PAD]
-            center = window[:, PAD : PAD + SPAN]
-            dx = along(center, 0)
-            dy = along(window, 1)[:, PAD : PAD + SPAN]
+    for m in range(4):
+        lanes = slice(SPAN * m, SPAN * m + SPAN)
+        inside = slice(PAD + SPAN * m, PAD + SPAN * m + SPAN)
+        for tile in range(4):
+            rows = slice(8 * tile, 8 * tile + 8)
             speeds = []
             for component in range(2):
-                tiles = []
-                for tile in range(4):
-                    bc = lambda j: jnp.broadcast_to(
-                        fine_y[plane, component, 8 * m + j : 8 * m + j + 1, :], (8, SPAN)
-                    )
-                    tiles.append(
-                        share_a * bc(max(2 * tile - 1, 0))
-                        + share_b * bc(2 * tile)
-                        + share_c * bc(2 * tile + 1)
-                    )
-                flow[component, :, lanes] = jnp.concatenate(tiles[1:3], 0)
-                speeds.append(jnp.concatenate(tiles, 0))
-            value = center - (speeds[0] * dx + speeds[1] * dy)
-            first[:, PAD + SPAN * m : PAD + SPAN * m + SPAN] = value
+                bc = lambda j: jnp.broadcast_to(
+                    fine_y[plane, component, 8 * m + j : 8 * m + j + 1, :], (8, SPAN)
+                )
+                speeds.append(
+                    share_a * bc(max(2 * tile - 1, 0))
+                    + share_b * bc(2 * tile)
+                    + share_c * bc(2 * tile + 1)
+                )
+                if tile in (1, 2):
+                    flow[component, 8 * tile - 8 : 8 * tile, lanes] = speeds[component]
+            value = field[plane, rows, inside] - (
+                speeds[0] * slope[plane, 0, rows, lanes] + speeds[1] * slope[plane, 1, rows, lanes]
+            )
+            first[rows, inside] = value
             if m == 0:
-                first[:, PAD + NF :] = value[:, :PAD]
+                first[rows, PAD + NF : NF + 2 * PAD] = value[:, :PAD]
             if m == 3:
-                first[:, 0:PAD] = value[:, SPAN - PAD :]
-        for m in range(4):
-            lanes = slice(SPAN * m, SPAN * m + SPAN)
-            window = first[:, SPAN * m : SPAN * m + SPAN + 2 * PAD]
-            center = window[:, PAD : PAD + SPAN]
-            dx = along(center, 0)[8:24]
-            dy = along(window[8:24], 1)[:, PAD : PAD + SPAN]
-            out[plane, :, lanes] = 0.5 * (
-                (scalar[plane, :, lanes] + center[8:24])
-                - (flow[0, :, lanes] * dx + flow[1, :, lanes] * dy)
-            )
-        return carry
-
-    lax.fori_loop(0, 4, plane_step, 0)
+                first[rows, 0:PAD] = value[:, SPAN - PAD :]
+    for m in range(4):
+        lanes = slice(SPAN * m, SPAN * m + SPAN)
+        window = first[:, SPAN * m : SPAN * m + SPAN + 2 * PAD]
+        center = window[:, PAD : PAD + SPAN]
+        dx = along(center, 0)[8:24]
+        dy = along(window[8:24], 1)[:, PAD : PAD + SPAN]
+        out[plane, :, lanes] = 0.5 * (
+            (field[plane, 8:24, PAD + SPAN * m : PAD + SPAN * m + SPAN] + center[8:24])
+            - (flow[0, :, lanes] * dx + flow[1, :, lanes] * dy)
+        )
+    return carry
 
 
 def spread_table():
@@ -376,17 +383,17 @@
     table, send, turn, weight = tables()
     dma = pltpu.SemaphoreType.DMA
     blocks = (OUTER, INNER)
-    next_coef, velocity, above, low, high = pl.pallas_call(
-        spectral_kernel,
+    return pl.pallas_call(
+        step_kernel,
         out_shape=(
             jax.ShapeDtypeStruct(velocity_coef.shape, F32),
-            jax.ShapeDtypeStruct((2, 8, NV), F32),
-            jax.ShapeDtypeStruct((2, 8, NV), F32),
-            jax.ShapeDtypeStruct((4, 8, NF), F32),
-            jax.ShapeDtypeStruct((4, 8, NF), F32),
+            jax.ShapeDtypeStruct(scalar_field.shape, F32),
         ),
-        in_specs=[vmem()] * 6,
-        out_specs=tuple([vmem()] * 5),
+        in_specs=[
+            pl.BlockSpec(memory_space=pltpu.SMEM), vmem(), pl.BlockSpec(memory_space=pl.ANY),
+            vmem(), vmem(), vmem(), vmem(), vmem(),
+        ],
+        out_specs=(vmem(), vmem()),
         scratch_shapes=[
             pltpu.VMEM((2, 256, 128), F32),
             pltpu.VMEM(blocks + (2, 128), F32),
@@ -396,28 +403,25 @@
             pltpu.VMEM(blocks + (1, 128), F32),
             pltpu.VMEM(blocks + (1, 128), F32),
             pltpu.VMEM(blocks + (1, 128), F32),
+            pltpu.VMEM((2, 8, NV), F32),
+            pltpu.VMEM((2, 8, NV), F32),
+            pltpu.VMEM((4, 32, NF + 2 * PAD), F32),
+            pltpu.VMEM((4, 2, 32, NF), F32),
+            pltpu.VMEM((32, NF + 2 * PAD), F32),
+            pltpu.VMEM((4, 2, 32, SPAN), F32),
+            pltpu.VMEM((2, 16, NF), F32),
             dma((6,)),
             dma((6,)),
             dma((4, 4)),
             dma((2,)),
+            dma((4,)),
         ],
         compiler_params=pltpu.CompilerParams(collective_id=0, has_side_effects=True),
-        name="spectral",
-    )(velocity_coef, scalar_field, jnp.asarray(table), jnp.asarray(send), jnp.asarray(turn), jnp.asarray(weight))
-    scalar_next = pl.pallas_call(
-        transport_kernel,
-        out_shape=jax.ShapeDtypeStruct(scalar_field.shape, F32),
-        in_specs=[pl.BlockSpec(memory_space=pltpu.SMEM)] + [vmem()] * 6,
-        out_specs=vmem(),
-        scratch_shapes=[
-            pltpu.VMEM((4, 32, NF + 2 * PAD), F32),
-            pltpu.VMEM((32, NF + 2 * PAD), F32),
-            pltpu.VMEM((4, 2, 32, 512), F32),
-            pltpu.VMEM((2, 16, NF), F32),
-        ],
-        name="transport",
-    )(plane_offset, scalar_field, low, high, velocity, above, jnp.asarray(spread_table(), jnp.bfloat16))
-    return next_coef, scalar_next
+        name="step",
+    )(
+        plane_offset, velocity_coef, scalar_field, jnp.asarray(table), jnp.asarray(send),
+        jnp.asarray(turn), jnp.asarray(weight), jnp.asarray(spread_table(), jnp.bfloat16),
+    )
 
 
 def solution(mesh):

time: 69.5 us -> 62.7 us (0.902)
  the two profiles are of different devices: /device:TPU:65 before, /device:TPU:1 now
where the time goes in v1:
time: 62.7 us; the launch traced here: 62.4 us
  Pallas kernels  58.5 us (93%)
  local copies, waits for them, and re-layouts  3.25 us (5%)
  between operations  0.64 us (1%)
    pallas_call x1, Pallas kernels, body(): pl.pallas_call(step_kernel, out_shape=(jax.ShapeDtypeStruct(velocity_coef...  58.5 us
    unnamed x2, local copies, waits for them, and re-layouts  3.25 us

profile of v1, /device:TPU:1, one launch (start us, length us, event | category | flops | bytes accessed | tf_op | source)
XLA Modules:
  0.0 62.4 jit_solution(15291304262482594712)
XLA Ops:
  0.6 58.5 %step.1 = (f32[2,2,1,4,512]{4,3,2,1,0:T(4,128)}, f32[4,16,2048]{2,1,0:T(8,128)}) custom-call(s32[4]{0:T(128)} %offset.1, f32[2,2,1,4,512]{4,3,2,1,0:T(4,128)} %coef.1, f32[4,16,2048]{2,1,0:T(8,128)} %scalar.1, f32[128,256]{1,0:T(8,128)} %constant.10.clone.table, f32[4,8,512]{2,1,0:T(8,128)} %constant.11.clone.send, f32[2,4,512]{2,1,0:T(4,128)} %constant.12.clone.turn, ...), custom_call_target="tpu_custom_call" | custom-call | tf_op jit(solution)/shard_map/step/pallas_call | solution.py:386
  59.1 1.4 %copy.12 = f32[2,2,1,4,512]{4,3,2,1,0:T(4,128)} copy(f32[2,2,1,4,512]{4,3,2,1,0:T(4,128)} %get-tuple-element.4) | data formatting | bytes 65536
  60.5 1.9 %copy.13 = f32[4,16,2048]{2,1,0:T(8,128)} copy(f32[4,16,2048]{2,1,0:T(8,128)} %get-tuple-element.5) | data formatting | bytes 1048576

commit v2 on v1

--- a/solution.py
+++ b/solution.py
@@ -11,11 +11,12 @@
 TIME_STEP = 0.05
 VISCOSITY = 0.5
 STENCIL = (0.8, -0.2, 4.0 / 105.0, -1.0 / 280.0)
-HIGHEST = lax.Precision.HIGHEST
+PRECISE = lax.Precision.HIGH
 MESH = pl.DeviceIdType.MESH
 NV = 512
 OUTER = 8
 INNER = 16
+COLUMNS, HALVES = 4, 2
 BLOCKS = OUTER * INNER
 F32 = jnp.float32
 PAD = 128
@@ -46,55 +47,87 @@
 
 def exchange(sent, passed, landed, sems, blk, grp):
     outer, inner = blk // INNER, blk % INNER
-
-    own = pltpu.make_async_copy(sent.at[outer], passed.at[outer], sems.at[0])
+    column, half = outer // HALVES, outer % HALVES
+    other = 1 - half
+
+    def to_column(there, side, group):
+        return pltpu.make_async_remote_copy(
+            sent.at[there, side], passed.at[half, column], sems.at[0, group], sems.at[1, group],
+            device_id=(grp, (there * HALVES + side) * INNER + inner), device_id_type=MESH,
+        )
+
+    def far(k, carry):
+        to_column(lax.rem(column + k, COLUMNS), other, 0).start()
+        return carry
+
+    def near(k, carry):
+        to_column(lax.rem(column + k, COLUMNS), half, 1).start()
+        return carry
+
+    lax.fori_loop(0, COLUMNS, far, 0)
+    own = pltpu.make_async_copy(sent.at[column, half], passed.at[half, column], sems.at[2, 0])
     own.start()
-
-    def first(k, carry):
-        there = lax.rem(outer + k, OUTER)
-        pltpu.make_async_remote_copy(
-            sent.at[there], passed.at[outer], sems.at[1], sems.at[2],
-            device_id=(grp, there * INNER + inner), device_id_type=MESH,
-        ).start()
-        return carry
-
-    lax.fori_loop(1, OUTER, first, 0)
-
-    def rest():
-        some = pl.ds(0, OUTER - 1)
-        every = pltpu.make_async_remote_copy(
-            sent.at[some], passed.at[some], sems.at[1], sems.at[2],
-            device_id=(grp, lax.rem(outer + 1, OUTER) * INNER + inner), device_id_type=MESH,
-        )
-        own.wait()
-        every.wait_recv()
-        mine = pltpu.make_async_copy(passed.at[:, inner], landed.at[:, inner], sems.at[3])
-        mine.start()
-
-        def second(k, carry):
+    lax.fori_loop(1, COLUMNS, near, 0)
+
+    def arrived(count, group):
+        some = pl.ds(0, count)
+        return pltpu.make_async_remote_copy(
+            passed.at[0, some], passed.at[0, some], sems.at[0, group], sems.at[1, group],
+            device_id=(grp, (lax.rem(column + 1, COLUMNS) * HALVES + half) * INNER + inner),
+            device_id_type=MESH,
+        )
+
+    def spread_inner(side, group):
+        mine = pltpu.make_async_copy(
+            passed.at[side, :, inner], landed.at[side, :, inner], sems.at[2, group]
+        )
+
+        def one(k, carry):
             there = lax.rem(inner + k, INNER)
             pltpu.make_async_remote_copy(
-                passed.at[:, there], landed.at[:, inner], sems.at[4], sems.at[5],
+                passed.at[side, :, there], landed.at[side, :, inner],
+                sems.at[0, group], sems.at[1, group],
                 device_id=(grp, outer * INNER + there), device_id_type=MESH,
             ).start()
             return carry
 
-        lax.fori_loop(1, INNER, second, 0)
-        every.wait_send()
-
-        def finish():
-            part = pl.ds(0, INNER - 1)
-            whole = pltpu.make_async_remote_copy(
-                passed.at[:, part], landed.at[:, part], sems.at[4], sems.at[5],
-                device_id=(grp, outer * INNER + lax.rem(inner + 1, INNER)), device_id_type=MESH,
-            )
-            mine.wait()
-            whole.wait_recv()
-            whole.wait_send()
-
-        return finish
-
-    return rest
+        lax.fori_loop(1, INNER, one, 0)
+        mine.start()
+        return mine
+
+    def landed_whole(side, group):
+        part = pl.ds(0, INNER - 1)
+        return pltpu.make_async_remote_copy(
+            passed.at[side, :, part], landed.at[side, :, part], sems.at[0, group], sems.at[1, group],
+            device_id=(grp, outer * INNER + lax.rem(inner + 1, INNER)), device_id_type=MESH,
+        )
+
+    def pass_near():
+        own.wait()
+        arrived(COLUMNS - 1, 1).wait_recv()
+        mine_near = spread_inner(half, 2)
+
+        def pass_far():
+            arrived(COLUMNS, 0).wait_recv()
+            mine_far = spread_inner(other, 3)
+
+            def finish():
+                mine_near.wait()
+                mine_far.wait()
+                landed_whole(half, 2).wait_recv()
+                landed_whole(other, 3).wait_recv()
+
+            def drain():
+                arrived(COLUMNS - 1, 1).wait_send()
+                arrived(COLUMNS, 0).wait_send()
+                landed_whole(half, 2).wait_send()
+                landed_whole(other, 3).wait_send()
+
+            return finish, drain
+
+        return pass_far
+
+    return pass_near
 
 
 def step_kernel(
@@ -156,13 +189,13 @@
             pack[0, pl.ds(start + 8, 8, 16), :] = im
             pack[1, pl.ds(start + 8, 8, 16), :] = re
     along_x = lax.dot_general(
-        table[...], jnp.concatenate([pack[0], pack[1]], 1), (((1,), (1,)), ((), ())), precision=HIGHEST,
+        table[...], jnp.concatenate([pack[0], pack[1]], 1), (((1,), (1,)), ((), ())), precision=PRECISE,
         preferred_element_type=F32,
     )
     for part in range(OUTER):
         rows = slice(part * INNER, part * INNER + INNER)
-        sent[part, :, 0, :] = along_x[rows, 0:128]
-        sent[part, :, 1, :] = along_x[rows, 128:256]
+        sent[part // HALVES, part % HALVES, :, 0, :] = along_x[rows, 0:128]
+        sent[part // HALVES, part % HALVES, :, 1, :] = along_x[rows, 128:256]
 
     pl.semaphore_wait(barrier, OUTER - 1 + INNER - 1 + 3)
 
@@ -181,12 +214,13 @@
         ))
     for copy in halos:
         copy.start()
-    step()()
-
-    vel_in = jnp.concatenate([landed[part, :, 0, :] for part in range(OUTER)], 0)
-    der_in = jnp.concatenate([landed[part, :, 1, :] for part in range(OUTER)], 0)
+    finish, drain = step()()
+    finish()
+
+    vel_in = jnp.concatenate([landed[part % HALVES, part // HALVES, :, 0, :] for part in range(OUTER)], 0)
+    der_in = jnp.concatenate([landed[part % HALVES, part // HALVES, :, 1, :] for part in range(OUTER)], 0)
     stacked = jnp.concatenate([vel_in.T, (vel_in * weight[...]).T, der_in.T], 0)
-    along_y = jnp.dot(stacked, table[...], precision=HIGHEST, preferred_element_type=F32)
+    along_y = jnp.dot(stacked, table[...], precision=PRECISE, preferred_element_type=F32)
 
     def synthesize(kind, component):
         parts = [0.0] * 4
@@ -237,23 +271,26 @@
             pack2[0, pl.ds(start + 8, 8, 16), :] = im
             pack2[1, pl.ds(start + 8, 8, 16), :] = -re
     forward_y = lax.dot_general(
-        table[...], jnp.concatenate([pack2[0], pack2[1]], 1), (((1,), (1,)), ((), ())), precision=HIGHEST,
+        table[...], jnp.concatenate([pack2[0], pack2[1]], 1), (((1,), (1,)), ((), ())), precision=PRECISE,
         preferred_element_type=F32,
     )
     for part in range(OUTER):
-        sent2[part, :, 0, :] = forward_y[part * INNER : part * INNER + INNER]
+        sent2[part // HALVES, part % HALVES, :, 0, :] = forward_y[part * INNER : part * INNER + INNER]
     step = exchange(sent2, passed2, landed2, sems2, blk, grp)
     for copy in own + halos:
         copy.wait()
     lax.fori_loop(0, 4, functools.partial(slopes, field, slope), 0)
-    finish = step()
-    lift.wait()
+    step = step()
+    lift.wait_recv()
     refine_along_y(offset, velocity, above, spread, fine_y)
-    lax.fori_loop(0, 4, functools.partial(sections, field, slope, first, fine_y, flow, out), 0)
-    finish()
-
-    back = jnp.concatenate([landed2[part, :, 0, :] for part in range(OUTER)], 0)
-    along = jnp.dot(back.T, table[...], precision=HIGHEST, preferred_element_type=F32)
+    transport = functools.partial(sections, field, slope, first, fine_y, flow, out)
+    lax.fori_loop(0, 2, transport, 0)
+    finish2, drain2 = step()
+    lax.fori_loop(2, 4, transport, 0)
+    finish2()
+
+    back = jnp.concatenate([landed2[part % HALVES, part // HALVES, :, 0, :] for part in range(OUTER)], 0)
+    along = jnp.dot(back.T, table[...], precision=PRECISE, preferred_element_type=F32)
     heads = []
     for row in range(1, 5):
         start = row * 16
@@ -286,6 +323,9 @@
             rows = slice(4 * component, 4 * component + 4)
             next_coef[component, 0, 0, :, lanes] = new_re[rows]
             next_coef[component, 1, 0, :, lanes] = new_im[rows]
+    lift.wait_send()
+    drain()
+    drain2()
 
 def refine_along_y(offset, velocity, above, spread, fine_y):
     for plane in range(4):
@@ -367,6 +407,21 @@
     return carry
 
 
+def place_kernel(coef, scalar, coef_out, scalar_out, coef_buffer, scalar_buffer, sems):
+    routes = [(coef, coef_buffer, coef_out)] + [
+        (scalar.at[plane], scalar_buffer.at[plane], scalar_out.at[plane]) for plane in range(4)
+    ]
+    loads = [pltpu.make_async_copy(a, b, sems.at[0, k]) for k, (a, b, c) in enumerate(routes)]
+    stores = [pltpu.make_async_copy(b, c, sems.at[1, k]) for k, (a, b, c) in enumerate(routes)]
+    for copy in loads:
+        copy.start()
+    for load, store in zip(loads, stores):
+        load.wait()
+        store.start()
+    for copy in stores:
+        copy.wait()
+
+
 def spread_table():
     fine = np.arange(512)
     table = np.zeros((256, 512), np.float32)
@@ -382,8 +437,7 @@
 def body(velocity_coef, scalar_field, plane_offset):
     table, send, turn, weight = tables()
     dma = pltpu.SemaphoreType.DMA
-    blocks = (OUTER, INNER)
-    return pl.pallas_call(
+    results = pl.pallas_call(
         step_kernel,
         out_shape=(
             jax.ShapeDtypeStruct(velocity_coef.shape, F32),
@@ -396,13 +450,13 @@
         out_specs=(vmem(), vmem()),
         scratch_shapes=[
             pltpu.VMEM((2, 256, 128), F32),
-            pltpu.VMEM(blocks + (2, 128), F32),
-            pltpu.VMEM(blocks + (2, 128), F32),
-            pltpu.VMEM(blocks + (2, 128), F32),
+            pltpu.VMEM((COLUMNS, HALVES, INNER, 2, 128), F32),
+            pltpu.VMEM((HALVES, COLUMNS, INNER, 2, 128), F32),
+            pltpu.VMEM((HALVES, COLUMNS, INNER, 2, 128), F32),
             pltpu.VMEM((2, 128, 128), F32),
-            pltpu.VMEM(blocks + (1, 128), F32),
-            pltpu.VMEM(blocks + (1, 128), F32),
-            pltpu.VMEM(blocks + (1, 128), F32),
+            pltpu.VMEM((COLUMNS, HALVES, INNER, 1, 128), F32),
+            pltpu.VMEM((HALVES, COLUMNS, INNER, 1, 128), F32),
+            pltpu.VMEM((HALVES, COLUMNS, INNER, 1, 128), F32),
             pltpu.VMEM((2, 8, NV), F32),
             pltpu.VMEM((2, 8, NV), F32),
             pltpu.VMEM((4, 32, NF + 2 * PAD), F32),
@@ -410,8 +464,8 @@
             pltpu.VMEM((32, NF + 2 * PAD), F32),
             pltpu.VMEM((4, 2, 32, SPAN), F32),
             pltpu.VMEM((2, 16, NF), F32),
-            dma((6,)),
-            dma((6,)),
+            dma((3, 4)),
+            dma((3, 4)),
             dma((4, 4)),
             dma((2,)),
             dma((4,)),
@@ -422,6 +476,22 @@
         plane_offset, velocity_coef, scalar_field, jnp.asarray(table), jnp.asarray(send),
         jnp.asarray(turn), jnp.asarray(weight), jnp.asarray(spread_table(), jnp.bfloat16),
     )
+    anywhere = pl.BlockSpec(memory_space=pl.ANY)
+    return pl.pallas_call(
+        place_kernel,
+        out_shape=(
+            jax.ShapeDtypeStruct(velocity_coef.shape, F32),
+            jax.ShapeDtypeStruct(scalar_field.shape, F32),
+        ),
+        in_specs=[anywhere, anywhere],
+        out_specs=(anywhere, anywhere),
+        scratch_shapes=[
+            pltpu.VMEM(velocity_coef.shape, F32),
+            pltpu.VMEM(scalar_field.shape, F32),
+            dma((2, 5)),
+        ],
+        name="place",
+    )(*results)
 
 
 def solution(mesh):

time: 62.7 us -> 60.6 us (0.967)
  local copies, waits for them, and re-layouts: 3.25 us -> 0 us
  Pallas kernels: 58.5 us -> 59.8 us
    unnamed x2 -> x0, local copies, waits for them, and re-layouts: 3.25 us -> none
    pallas_call x0 -> x1, Pallas kernels: none -> 1.86 us  [body(): pl.pallas_call(place_kernel, out_shape=(jax.ShapeDtypeStruct(velocity_coe...]
where the time goes in v2:
time: 60.6 us; the launch traced here: 60.4 us
  Pallas kernels  59.8 us (99%)
  between operations  0.64 us (1%)
    pallas_call x1, Pallas kernels, body(): pl.pallas_call(step_kernel, out_shape=(jax.ShapeDtypeStruct(velocity_coef...  57.9 us
    pallas_call x1, Pallas kernels, body(): pl.pallas_call(place_kernel, out_shape=(jax.ShapeDtypeStruct(velocity_coe...  1.86 us

profile of v2, /device:TPU:1, one launch (start us, length us, event | category | flops | bytes accessed | tf_op | source)
XLA Modules:
  0.0 60.4 jit_solution(12400478995121417608)
XLA Ops:
  0.6 57.9 %step.1 = (f32[2,2,1,4,512]{4,3,2,1,0:T(4,128)}, f32[4,16,2048]{2,1,0:T(8,128)}) custom-call(s32[4]{0:T(128)} %offset.1, f32[2,2,1,4,512]{4,3,2,1,0:T(4,128)} %coef.1, f32[4,16,2048]{2,1,0:T(8,128)} %scalar.1, f32[128,256]{1,0:T(8,128)} %constant.10.clone.table, f32[4,8,512]{2,1,0:T(8,128)} %constant.11.clone.send, f32[2,4,512]{2,1,0:T(4,128)} %constant.12.clone.turn, ...), custom_call_target="tpu_custom_call" | custom-call | tf_op jit(solution)/shard_map/step/pallas_call | solution.py:440
  58.6 1.9 %place.1 = (f32[2,2,1,4,512]{4,3,2,1,0:T(4,128)}, f32[4,16,2048]{2,1,0:T(8,128)}) custom-call(f32[2,2,1,4,512]{4,3,2,1,0:T(4,128)} %get-tuple-element.4.coef, f32[4,16,2048]{2,1,0:T(8,128)} %get-tuple-element.5.scalar), custom_call_target="tpu_custom_call" | custom-call | tf_op jit(solution)/shard_map/place/pallas_call | solution.py:480

commit v3 on v2

--- a/solution.py
+++ b/solution.py
@@ -57,7 +57,7 @@
         )
 
     def far(k, carry):
-        to_column(lax.rem(column + k, COLUMNS), other, 0).start()
+        to_column(lax.rem(column + 2 + k, COLUMNS), other, 0).start()
         return carry
 
     def near(k, carry):
@@ -131,11 +131,12 @@
 
 
 def step_kernel(
-    offset, coef, scalar, table, send, turn, weight, spread,
+    offset, coef_in, scalar, table_in, send_in, turn_in, weight_in, spread_in,
     next_coef, out,
     pack, sent, passed, landed, pack2, sent2, passed2, landed2,
     velocity, above, field, slope, first, fine_y, flow,
-    sems, sems2, halo_sems, grp_sems, own_sem,
+    coef, table, send, turn, weight, spread, ready,
+    sems, sems2, halo_sems, grp_sems, own_sem, load_sem, out_sem,
 ):
     blk = lax.axis_index("blk")
     grp = lax.axis_index("grp")
@@ -144,23 +145,40 @@
     groups = lax.axis_size("grp")
     below, upper = lax.rem(grp + groups - 1, groups), lax.rem(grp + 1, groups)
 
+    loads = [
+        pltpu.make_async_copy(source, target, load_sem.at[k])
+        for k, (source, target) in enumerate((
+            (coef_in, coef), (send_in, send), (table_in, table),
+            (weight_in, weight), (turn_in, turn), (spread_in, spread),
+        ))
+    ]
+    for copy in loads:
+        copy.start()
+
     barrier = pltpu.get_barrier_semaphore()
 
     def hello(device):
         pl.semaphore_signal(barrier, inc=1, device_id=device, device_id_type=MESH)
 
-    def greet_outer(k, carry):
-        hello((grp, lax.rem(outer + k, OUTER) * INNER + inner))
+    column, side = outer // HALVES, outer % HALVES
+
+    def greet_far(k, carry):
+        hello((grp, (lax.rem(column + 2 + k, COLUMNS) * HALVES + 1 - side) * INNER + inner))
+        return carry
+
+    def greet_near(k, carry):
+        hello((grp, (lax.rem(column + k, COLUMNS) * HALVES + side) * INNER + inner))
         return carry
 
     def greet_inner(k, carry):
         hello((grp, outer * INNER + lax.rem(inner + k, INNER)))
         return carry
 
+    lax.fori_loop(0, COLUMNS, greet_far, 0)
     hello((grp, behind))
     hello((grp, ahead))
     hello((upper, blk))
-    lax.fori_loop(1, OUTER, greet_outer, 0)
+    lax.fori_loop(1, COLUMNS, greet_near, 0)
     lax.fori_loop(1, INNER, greet_inner, 0)
     whole = pl.ds(PAD, NF)
     own = [
@@ -171,6 +189,9 @@
     ]
     for copy in own:
         copy.start()
+
+    for copy in loads:
+        copy.wait()
 
     real = jnp.concatenate([coef[0, 0, 0], coef[1, 0, 0]], 0)
     imag = jnp.concatenate([coef[0, 1, 0], coef[1, 1, 0]], 0)
@@ -277,16 +298,28 @@
     for part in range(OUTER):
         sent2[part // HALVES, part % HALVES, :, 0, :] = forward_y[part * INNER : part * INNER + INNER]
     step = exchange(sent2, passed2, landed2, sems2, blk, grp)
-    for copy in own + halos:
-        copy.wait()
-    lax.fori_loop(0, 4, functools.partial(slopes, field, slope), 0)
     step = step()
+    late = (inner == 0) | (inner == INNER - 1)
+
+    def with_halo():
+        for copy in own + halos:
+            copy.wait()
+        lax.fori_loop(0, 4, functools.partial(slopes, field, slope), 0)
+
+    pl.when(jnp.logical_not(late))(with_halo)
     lift.wait_recv()
     refine_along_y(offset, velocity, above, spread, fine_y)
-    transport = functools.partial(sections, field, slope, first, fine_y, flow, out)
-    lax.fori_loop(0, 2, transport, 0)
+
+    def transport(plane, carry):
+        sections(field, slope, first, fine_y, flow, ready, plane, carry)
+        pltpu.make_async_copy(ready.at[plane], out.at[plane], out_sem.at[plane]).start()
+        return carry
+
+    done = jnp.where(late, 0, 2)
+    lax.fori_loop(0, done, transport, 0)
     finish2, drain2 = step()
-    lax.fori_loop(2, 4, transport, 0)
+    pl.when(late)(with_halo)
+    lax.fori_loop(done, 4, transport, 0)
     finish2()
 
     back = jnp.concatenate([landed2[part % HALVES, part // HALVES, :, 0, :] for part in range(OUTER)], 0)
@@ -323,6 +356,8 @@
             rows = slice(4 * component, 4 * component + 4)
             next_coef[component, 0, 0, :, lanes] = new_re[rows]
             next_coef[component, 1, 0, :, lanes] = new_im[rows]
+    for plane in range(4):
+        pltpu.make_async_copy(ready.at[plane], out.at[plane], out_sem.at[plane]).wait()
     lift.wait_send()
     drain()
     drain2()
@@ -437,6 +472,7 @@
 def body(velocity_coef, scalar_field, plane_offset):
     table, send, turn, weight = tables()
     dma = pltpu.SemaphoreType.DMA
+    anywhere = pl.BlockSpec(memory_space=pl.ANY)
     results = pl.pallas_call(
         step_kernel,
         out_shape=(
@@ -444,10 +480,10 @@
             jax.ShapeDtypeStruct(scalar_field.shape, F32),
         ),
         in_specs=[
-            pl.BlockSpec(memory_space=pltpu.SMEM), vmem(), pl.BlockSpec(memory_space=pl.ANY),
-            vmem(), vmem(), vmem(), vmem(), vmem(),
+            pl.BlockSpec(memory_space=pltpu.SMEM), anywhere, anywhere,
+            anywhere, anywhere, anywhere, anywhere, anywhere,
         ],
-        out_specs=(vmem(), vmem()),
+        out_specs=(vmem(), anywhere),
         scratch_shapes=[
             pltpu.VMEM((2, 256, 128), F32),
             pltpu.VMEM((COLUMNS, HALVES, INNER, 2, 128), F32),
@@ -464,10 +500,19 @@
             pltpu.VMEM((32, NF + 2 * PAD), F32),
             pltpu.VMEM((4, 2, 32, SPAN), F32),
             pltpu.VMEM((2, 16, NF), F32),
+            pltpu.VMEM(velocity_coef.shape, F32),
+            pltpu.VMEM(table.shape, F32),
+            pltpu.VMEM(send.shape, F32),
+            pltpu.VMEM(turn.shape, F32),
+            pltpu.VMEM(weight.shape, F32),
+            pltpu.VMEM((256, 512), jnp.bfloat16),
+            pltpu.VMEM(scalar_field.shape, F32),
             dma((3, 4)),
             dma((3, 4)),
             dma((4, 4)),
             dma((2,)),
+            dma((4,)),
+            dma((6,)),
             dma((4,)),
         ],
         compiler_params=pltpu.CompilerParams(collective_id=0, has_side_effects=True),
@@ -476,7 +521,6 @@
         plane_offset, velocity_coef, scalar_field, jnp.asarray(table), jnp.asarray(send),
         jnp.asarray(turn), jnp.asarray(weight), jnp.asarray(spread_table(), jnp.bfloat16),
     )
-    anywhere = pl.BlockSpec(memory_space=pl.ANY)
     return pl.pallas_call(
         place_kernel,
         out_shape=(

time: 60.6 us -> 60.7 us (level)
  no operation moved by 1% of the time
where the time goes in v3:
time: 60.7 us; the launch traced here: 60.5 us
  Pallas kernels  59.9 us (99%)
  between operations  0.64 us (1%)
    pallas_call x1, Pallas kernels, body(): pl.pallas_call(step_kernel, out_shape=(jax.ShapeDtypeStruct(velocity_coef...  58.1 us
    pallas_call x1, Pallas kernels, body(): pl.pallas_call(place_kernel, out_shape=(jax.ShapeDtypeStruct(velocity_coe...  1.86 us

profile of v3, /device:TPU:1, one launch (start us, length us, event | category | flops | bytes accessed | tf_op | source)
XLA Modules:
  0.0 60.5 jit_solution(7791700280545625322)
XLA Ops:
  0.6 58.1 %step.1 = (f32[2,2,1,4,512]{4,3,2,1,0:T(4,128)}, f32[4,16,2048]{2,1,0:T(8,128)}) custom-call(s32[4]{0:T(128)} %offset.1, f32[2,2,1,4,512]{4,3,2,1,0:T(4,128)} %coef_in.1, f32[4,16,2048]{2,1,0:T(8,128)} %scalar.1, f32[128,256]{1,0:T(8,128)} %constant.10.clone.table_in, f32[4,8,512]{2,1,0:T(8,128)} %constant.11.clone.send_in, ...), custom_call_target="tpu_custom_call" | custom-call | tf_op jit(solution)/shard_map/step/pallas_call | solution.py:476
  58.7 1.9 %place.1 = (f32[2,2,1,4,512]{4,3,2,1,0:T(4,128)}, f32[4,16,2048]{2,1,0:T(8,128)}) custom-call(f32[2,2,1,4,512]{4,3,2,1,0:T(4,128)} %get-tuple-element.4.coef, f32[4,16,2048]{2,1,0:T(8,128)} %get-tuple-element.5.scalar), custom_call_target="tpu_custom_call" | custom-call | tf_op jit(solution)/shard_map/place/pallas_call | solution.py:524

commit v4 on v3

--- a/solution.py
+++ b/solution.py
@@ -442,17 +442,13 @@
     return carry
 
 
-def place_kernel(coef, scalar, coef_out, scalar_out, coef_buffer, scalar_buffer, sems):
-    routes = [(coef, coef_buffer, coef_out)] + [
-        (scalar.at[plane], scalar_buffer.at[plane], scalar_out.at[plane]) for plane in range(4)
+def place_kernel(coef, scalar, coef_out, scalar_out, sems):
+    stores = [pltpu.make_async_copy(coef, coef_out, sems.at[4])] + [
+        pltpu.make_async_copy(scalar.at[plane], scalar_out.at[plane], sems.at[plane])
+        for plane in range(4)
     ]
-    loads = [pltpu.make_async_copy(a, b, sems.at[0, k]) for k, (a, b, c) in enumerate(routes)]
-    stores = [pltpu.make_async_copy(b, c, sems.at[1, k]) for k, (a, b, c) in enumerate(routes)]
-    for copy in loads:
+    for copy in stores:
         copy.start()
-    for load, store in zip(loads, stores):
-        load.wait()
-        store.start()
     for copy in stores:
         copy.wait()
 
@@ -480,8 +476,7 @@
             jax.ShapeDtypeStruct(scalar_field.shape, F32),
         ),
         in_specs=[
-            pl.BlockSpec(memory_space=pltpu.SMEM), anywhere, anywhere,
-            anywhere, anywhere, anywhere, anywhere, anywhere,
+            pl.BlockSpec(memory_space=pltpu.SMEM), *[pl.BlockSpec(memory_space=pltpu.HBM)] * 7,
         ],
         out_specs=(vmem(), anywhere),
         scratch_shapes=[
@@ -515,11 +510,18 @@
             dma((6,)),
             dma((4,)),
         ],
-        compiler_params=pltpu.CompilerParams(collective_id=0, has_side_effects=True),
+        compiler_params=pltpu.CompilerParams(
+            collective_id=0, has_side_effects=True, vmem_limit_bytes=12 << 20
+        ),
         name="step",
     )(
-        plane_offset, velocity_coef, scalar_field, jnp.asarray(table), jnp.asarray(send),
-        jnp.asarray(turn), jnp.asarray(weight), jnp.asarray(spread_table(), jnp.bfloat16),
+        plane_offset, *[
+            pltpu.with_memory_space_constraint(array, pltpu.HBM)
+            for array in (
+                velocity_coef, scalar_field, jnp.asarray(table), jnp.asarray(send),
+                jnp.asarray(turn), jnp.asarray(weight), jnp.asarray(spread_table(), jnp.bfloat16),
+            )
+        ],
     )
     return pl.pallas_call(
         place_kernel,
@@ -529,11 +531,8 @@
         ),
         in_specs=[anywhere, anywhere],
         out_specs=(anywhere, anywhere),
-        scratch_shapes=[
-            pltpu.VMEM(velocity_coef.shape, F32),
-            pltpu.VMEM(scalar_field.shape, F32),
-            dma((2, 5)),
-        ],
+        scratch_shapes=[dma((5,))],
+        compiler_params=pltpu.CompilerParams(vmem_limit_bytes=4 << 20),
         name="place",
     )(*results)
 

time: 60.7 us -> 59.6 us (0.982)
  Pallas kernels: 59.9 us -> 58.2 us
  local copies, waits for them, and re-layouts: 0 us -> 0.65 us
    pallas_call x1, Pallas kernels: 1.86 us -> 0.84 us  [body(): pl.pallas_call(place_kernel, out_shape=(jax.ShapeDtypeStruct(velocity_coe...]
    pallas_call x1, Pallas kernels: 58.1 us -> 57.3 us  [body(): pl.pallas_call(step_kernel, out_shape=(jax.ShapeDtypeStruct(velocity_coef...]
    unnamed x0 -> x2, local copies, waits for them, and re-layouts: none -> 0.65 us
where the time goes in v4:
time: 59.6 us; the launch traced here: 59.4 us
  Pallas kernels  58.2 us (98%)
  local copies, waits for them, and re-layouts  0.65 us (1%)
  between operations  0.65 us (1%)
    pallas_call x1, Pallas kernels, body(): pl.pallas_call(step_kernel, out_shape=(jax.ShapeDtypeStruct(velocity_coef...  57.3 us

profile of v4, /device:TPU:1, one launch (start us, length us, event | category | flops | bytes accessed | tf_op | source)
XLA Modules:
  0.0 59.4 jit_solution(10315696556928268096)
XLA Ops:
  0.6 0.0 copy-start
  0.6 0.6 %copy-done = s32[4]{0:T(128)S(1)} copy-done((s32[4]{0:T(128)S(1)}, s32[4]{0:T(128)}, u32[]{:S(2)}) %copy-start) | copy-done | bytes 40
  1.3 57.3 %step.1 = (f32[2,2,1,4,512]{4,3,2,1,0:T(4,128)S(1)}, f32[4,16,2048]{2,1,0:T(8,128)S(1)}) custom-call(s32[4]{0:T(128)S(1)} %copy-done, f32[2,2,1,4,512]{4,3,2,1,0:T(4,128)} %coef_in.1, f32[4,16,2048]{2,1,0:T(8,128)} %scalar.1, f32[128,256]{1,0:T(8,128)} %constant.10.clone.table_in, f32[4,8,512]{2,1,0:T(8,128)} %constant.11.clone.send_in, ...), custom_call_target="tpu_custom_call" | custom-call | tf_op jit(solution)/shard_map/step/pallas_call | solution.py:472
  58.6 0.8 %place.1 = (f32[2,2,1,4,512]{4,3,2,1,0:T(4,128)}, f32[4,16,2048]{2,1,0:T(8,128)}) custom-call(f32[2,2,1,4,512]{4,3,2,1,0:T(4,128)S(1)} %get-tuple-element.4.coef, f32[4,16,2048]{2,1,0:T(8,128)S(1)} %get-tuple-element.5.scalar), custom_call_target="tpu_custom_call" | custom-call | tf_op jit(solution)/shard_map/place/pallas_call | solution.py:526
Async XLA Ops:
  0.6 0.7 %copy-start = (s32[4]{0:T(128)S(1)}, s32[4]{0:T(128)}, u32[]{:S(2)}) copy-start(s32[4]{0:T(128)} %offset.1) | copy-start | bytes 52
